TPU v7x, 32 devices: a whole 2x2x4 slice. The times are simulated.
32 devices in a mesh: section: 4 (over y, x), dp: 8 (over z, core).
Axes of the slice: x: 2, y: 2, z: 4, core: 2. Of those that a mesh axis runs over, the one named last changes fastest.
Arguments:
- images: bfloat16 [4, 8, 8, 16, 768], P(None, 'dp'), may hold values from -6 to 6
- widths: int32 [4], replicated, may hold values from 0 to 2, as said below
- depth_kernel: bfloat16 [4, 7, 7, 768], P('section'), may hold values from -0.875 to 0.875
- depth_bias: bfloat16 [4, 768], P('section'), may hold values from -3 to 3
- ln_gain: bfloat16 [4, 768], P('section'), may hold values from 0.25 to 1.75
- ln_bias: bfloat16 [4, 768], P('section'), may hold values from -3 to 3
- w_in: bfloat16 [4, 1536, 768], P('section', 'dp'), may hold values from -0.21875 to 0.21875
- w_out: bfloat16 [4, 1536, 768], P('section', 'dp'), may hold values from -0.15625 to 0.15625
- layer_scale: bfloat16 [4, 768], P('section'), may hold values from 0.29882812 to 1
Outputs:
- section_acts: bfloat16 [4, 4, 8, 8, 16, 768], P('section', None, 'dp')
Inputs may be any that keep to these rules, and one draw needn't show every extreme that they name: `widths`: each half of the micro-batches holds exactly one at level 0 and one at a level above 0; levels 1 and 2 both appear.
All inputs are finite; a program needn't handle non-finite values.
Results may differ from a plain program's by a relative error of at most 0.0065.
Values may be sent and summed in bfloat16 or wider, within the bound.
A program may use at most 64 MiB of HBM per device.

v0:
```python
import jax
import jax.numpy as jnp
from jax import lax
from jax.sharding import PartitionSpec as P


def swapped(value, axis, stride):
    mask = 2**stride
    pairs = [(source, source ^ mask) for source in range(lax.axis_size(axis))]
    return lax.ppermute(value, axis, pairs)


def passed_along(value, axis, steps):
    count = lax.axis_size(axis)
    initial, last = (max(0, -steps), min(count, count - steps))
    return lax.ppermute(value, axis, [(source, source + steps) for source in range(initial, last)])


def conv_block(
    inputs, width_level, depth_kernel, depth_bias, ln_gain, ln_bias, w_in, w_out, layer_scale
):
    channels = inputs.shape[-1]
    hidden = w_in.shape[0]
    active_channels = jnp.where(
        width_level == 0, channels, jnp.where(width_level == 1, channels // 2, channels // 4)
    )
    active_hidden = jnp.where(
        width_level == 0, hidden, jnp.where(width_level == 1, hidden // 2, hidden // 4)
    )
    chan_mask = (jnp.arange(channels) < active_channels).astype(jnp.float32)
    hidden_mask = (jnp.arange(hidden) < active_hidden).astype(jnp.float32)
    channel_count = active_channels.astype(jnp.float32)
    widened = inputs.astype(jnp.float32) * chan_mask
    kernel = depth_kernel.astype(jnp.float32)
    reach = kernel.shape[0] // 2
    padded = jnp.pad(widened, ((0, 0), (reach, reach), (reach, reach), (0, 0)))
    rows_n = inputs.shape[1]
    cols_n = inputs.shape[2]
    spatial = jnp.zeros(widened.shape, jnp.float32)
    for row_off in range(kernel.shape[0]):
        for col_off in range(kernel.shape[1]):
            spatial = (
                spatial
                + padded[:, row_off : row_off + rows_n, col_off : col_off + cols_n, :]
                * kernel[row_off, col_off]
            )
    spatial = (spatial + depth_bias.astype(jnp.float32)) * chan_mask
    average = jnp.sum(spatial, axis=-1, keepdims=True) / channel_count
    centred = (spatial - average) * chan_mask
    variance = jnp.sum(centred * centred, axis=-1, keepdims=True) / channel_count
    normed = (
        centred * lax.rsqrt(variance + 1e-06) * ln_gain.astype(jnp.float32)
        + ln_bias.astype(jnp.float32)
    ) * chan_mask
    flattened = normed.astype(jnp.bfloat16).reshape(-1, channels)
    expanded = jnp.dot(flattened, w_in.T, preferred_element_type=jnp.float32)
    activated = (jax.nn.gelu(expanded, approximate=True) * hidden_mask).astype(jnp.bfloat16)
    projected = jnp.dot(activated, w_out, preferred_element_type=jnp.float32).reshape(widened.shape)
    result = widened + layer_scale.astype(jnp.float32) * projected * chan_mask
    return result.astype(jnp.bfloat16)


def run_slot(
    stored, received, tick_index, offset, entry_first, base_slot, count, images, widths, parameters
):
    slot_index = tick_index - offset
    is_live = (slot_index >= 0) & (slot_index < count)
    clipped = jnp.clip(slot_index, 0, count - 1) + base_slot
    entering = lax.dynamic_index_in_dim(images, clipped, 0, keepdims=False)
    source = jnp.where(entry_first, entering, received)
    width_level = widths[clipped]
    result = lax.cond(
        is_live,
        lambda operand: conv_block(operand, width_level, *parameters),
        lambda operand: jnp.zeros_like(operand),
        source,
    )
    previous = lax.dynamic_index_in_dim(stored, clipped, 0, keepdims=False)
    stored = lax.dynamic_update_index_in_dim(
        stored, jnp.where(is_live, result, previous), clipped, 0
    )
    return (stored, result)


def on_device(images, widths, depth_kernel, depth_bias, ln_gain, ln_bias, w_in, w_out, layer_scale):
    sections = lax.axis_size("section")
    position = lax.axis_index("section")
    microbatches = images.shape[0]
    halfway = microbatches // 2
    bit_total = sections.bit_length() - 1
    stored = jnp.zeros(images.shape, jnp.bfloat16)
    empty_tile = jnp.zeros(images.shape[1:], jnp.bfloat16)
    shards = (w_in, w_out, depth_kernel, depth_bias, ln_gain, ln_bias, layer_scale)
    for bit_index in range(bit_total):
        shards = swapped(
            (shards[0], shards[1], shards[2], shards[3], shards[4], shards[5], shards[6]),
            "section",
            bit_index,
        )
    full_in, full_out, mirror_in, mirror_out = (
        lax.all_gather(w_in, "dp", axis=1, tiled=True),
        lax.all_gather(w_out, "dp", axis=1, tiled=True),
        lax.all_gather(shards[0], "dp", axis=1, tiled=True),
        lax.all_gather(shards[1], "dp", axis=1, tiled=True),
    )
    own_params = (
        depth_kernel[0],
        depth_bias[0],
        ln_gain[0],
        ln_bias[0],
        full_in[0],
        full_out[0],
        layer_scale[0],
    )
    mirror_params = (
        shards[2][0],
        shards[3][0],
        shards[4][0],
        shards[5][0],
        mirror_in[0],
        mirror_out[0],
        shards[6][0],
    )
    tick_total = sections - 1 + halfway

    def advance(tick_index, carried):
        down_received, up_received, kept = carried
        kept, down_result = run_slot(
            kept,
            down_received,
            tick_index,
            position,
            position == 0,
            0,
            halfway,
            images,
            widths,
            own_params,
        )
        kept, up_result = run_slot(
            kept,
            up_received,
            tick_index,
            sections - 1 - position,
            position == sections - 1,
            halfway,
            halfway,
            images,
            widths,
            mirror_params,
        )
        down_received = passed_along(down_result, "section", 1)
        up_received = passed_along(up_result, "section", -1)
        return (down_received, up_received, kept)

    _, _, stored = lax.fori_loop(0, tick_total, advance, (empty_tile, empty_tile, stored))
    return stored[None]


def solution(mesh):
    placed = (
        P(None, "dp", None, None, None),
        P(),
        P("section", None, None, None),
        P("section", None),
        P("section", None),
        P("section", None),
        P("section", "dp", None),
        P("section", "dp", None),
        P("section", None),
    )
    return jax.shard_map(
        on_device,
        mesh=mesh,
        in_specs=placed,
        out_specs=P("section", None, "dp", None, None, None),
        check_vma=False,
    )
```

profile of v0, /device:TPU:6, one launch (start us, length us, event | category | flops | bytes accessed | tf_op | source)
XLA Modules:
  0.0 269.6 jit_solution(6992223651188118496)
XLA Ops:
  6.5 0.7 all-gather.5.cloned.1.call-update
  8.7 8.4 %collective-permute-done.12 = bf16[1,192,768]{2,1,0:T(8,128)(2,1)S(1)} collective-permute-done((bf16[1,192,768]{2,1,0:T(8,128)(2,1)}, bf16[1,192,768]{2,1,0:T(8,128)(2,1)S(1)}, u32[]{:S(2)}, u32[]{:S(2)}) %collective-permute-start.12) | collective-permute-done | bytes 294944 | tf_op jit(solution)/shard_map/ppermute | solution.py:10
  17.6 7.4 %collective-permute-done.13 = bf16[1,192,768]{2,1,0:T(8,128)(2,1)S(1)} collective-permute-done((bf16[1,192,768]{2,1,0:T(8,128)(2,1)S(1)}, bf16[1,192,768]{2,1,0:T(8,128)(2,1)S(1)}, u32[]{:S(2)}, u32[]{:S(2)}) %collective-permute-start.13) | collective-permute-done | bytes 294944 | tf_op jit(solution)/shard_map/ppermute | solution.py:10
  25.0 0.7 copy-done.3
  26.4 6.8 %collective-permute-done.14 = bf16[1,192,768]{2,1,0:T(8,128)(2,1)S(1)} collective-permute-done((bf16[1,192,768]{2,1,0:T(8,128)(2,1)}, bf16[1,192,768]{2,1,0:T(8,128)(2,1)S(1)}, u32[]{:S(2)}, u32[]{:S(2)}) %collective-permute-start.14) | collective-permute-done | bytes 294944 | tf_op jit(solution)/shard_map/ppermute | solution.py:10
  33.7 6.2 %collective-permute-done.15 = bf16[1,192,768]{2,1,0:T(8,128)(2,1)S(1)} collective-permute-done((bf16[1,192,768]{2,1,0:T(8,128)(2,1)S(1)}, bf16[1,192,768]{2,1,0:T(8,128)(2,1)S(1)}, u32[]{:S(2)}, u32[]{:S(2)}) %collective-permute-start.15) | collective-permute-done | bytes 294944 | tf_op jit(solution)/shard_map/ppermute | solution.py:10
  41.2 4.2 %collective-permute-done.4 = bf16[1,7,7,768]{3,2,1,0:T(8,128)(2,1)S(1)} collective-permute-done((bf16[1,7,7,768]{3,2,1,0:T(8,128)(2,1)}, bf16[1,7,7,768]{3,2,1,0:T(8,128)(2,1)S(1)}, u32[]{:S(2)}, u32[]{:S(2)}) %collective-permute-start.4) | collective-permute-done | bytes 75296 | tf_op jit(solution)/shard_map/ppermute | solution.py:10
  46.0 0.8 collective-permute-start.2
  46.8 1.2 collective-permute-start.6
  48.0 0.8 collective-permute-start.8
  48.8 1.2 collective-permute-start.10
  50.0 1.5 collective-permute-start.3
  52.1 1.5 collective-permute-start.9
  57.2 16.8 %all-gather.7.cloned.1.call-done = bf16[1,1536,768]{2,1,0:T(8,128)(2,1)} async-done(((bf16[1,192,768]{2,1,0:T(8,128)(2,1)}), bf16[1,1536,768]{2,1,0:T(8,128)(2,1)}) %all-gather.7.cloned.1.call-update) | async-done | bytes 2359312 | tf_op jit(solution)/shard_map/all_gather | solution.py:102
  74.0 32.4 %all-gather.9.cloned.1.call-done = bf16[1,1536,768]{2,1,0:T(8,128)(2,1)} async-done(((bf16[1,192,768]{2,1,0:T(8,128)(2,1)}), bf16[1,1536,768]{2,1,0:T(8,128)(2,1)}) %all-gather.9.cloned.1.call-update) | async-done | bytes 2359312 | tf_op jit(solution)/shard_map/all_gather | solution.py:103
  106.4 32.2 %all-gather.11.cloned.1.call-done = bf16[1,1536,768]{2,1,0:T(8,128)(2,1)} async-done(((bf16[1,192,768]{2,1,0:T(8,128)(2,1)}), bf16[1,1536,768]{2,1,0:T(8,128)(2,1)}) %all-gather.11.cloned.1.call-update) | async-done | bytes 2359312 | tf_op jit(solution)/shard_map/all_gather | solution.py:104
  138.7 123.5 %while.19 = (s32[]{:T(128)}, bf16[1,8,16,768]{3,2,1,0:T(8,128)(2,1)S(1)}, bf16[1,8,16,768]{3,2,1,0:T(8,128)(2,1)S(1)}, bf16[4,1,8,16,768]{4,3,2,1,0:T(8,128)(2,1...) while((s32[]{:T(128)}, ...), condition=%wide.region_9.10_spmd, body=%wide.region_0.9_spmd.sunk | while | flops 1235378944 | bytes 22721452 | solution.py:156
  138.8 10.3 %conditional.5 = (bf16[1,8,16,768]{3,2,1,0:T(8,128)(2,1)S(1)}) conditional(s32[]{:T(128)} %convert_element_type.176, () %tuple.160, (pred[]{:T(512)}, bf16[4,1,8,16,768]{4,3,2,1,0:T(8,128)(2,1)S(1)}, s32[]{:T(128)}, bf16[1,8,16,768]{3,2,1,0:T(8,128)(2,1)S(1)}, s32[4]{0:T(128)S(1)}, /*index=5*/bf16[768]{0:T(1024)(128)(2,1)S(1)}, ...), branch_computations={%region_5.5_spmd, %region_6.8_spmd} | conditional | flops 617591168 | bytes 9590903 | solution.py:72
  141.4 3.5 %fusion.242 = (f32[8,16]{1,0:T(8,128)S(1)}, f32[1,8,16,768]{3,2,1,0:T(8,128)S(1)}) fusion(f32[768]{0:T(1024)S(1)} %fusion.235, f32[768]{0:T(1024)S(1)} %convert_element_type.149, f32[768]{0:T(1024)S(1)} %get-tuple-element.768, f32[768]{0:T(1024)S(1)} %get-tuple-element.769, f32[768]{0:T(1024)S(1)} %get-tuple-element.770, f32[768]{0:T(1024)S(1)} %get-tuple-element.771, ...), kind=kLoop, calls=%fused_computation.461 | loop fusion | flops 9830272 | bytes 943616 | tf_op jit(solution)/shard_map/while/body/eval_jaxpr/cond/branch_1_fun/reduce_sum | solution.py:48
  145.3 3.7 %fusion.129 = f32[128,768]{1,0:T(8,128)S(1)} fusion(bf16[1536,768]{1,0:T(8,128)(2,1)} %get-tuple-element.690, f32[1536]{0:T(1024)S(1)} %fusion.234, bf16[128,768]{1,0:T(8,128)(2,1)S(1)} %bitcast.51, bf16[1536,768]{1,0:T(8,128)(2,1)} %get-tuple-element.689), kind=kOutput, calls=%fused_computation.285 | convolution fusion | flops 605945856 | bytes 5314560 | tf_op jit(solution)/shard_map/while/body/eval_jaxpr/cond/branch_1_fun/dot_general | solution.py:58
  149.0 1.3 collective-permute-start.1
  150.4 1.3 collective-permute-start
  151.9 3.3 %collective-permute-done.1 = bf16[1,8,16,768]{3,2,1,0:T(8,128)(2,1)S(1)} collective-permute-done((bf16[1,8,16,768]{3,2,1,0:T(8,128)(2,1)S(1)}, bf16[1,8,16,768]{3,2,1,0:T(8,128)(2,1)S(1)}, u32[]{:S(2)}, u32[]{:S(2)}) %collective-permute-start.1) | collective-permute-done | bytes 196640 | tf_op jit(solution)/shard_map/while/body/eval_jaxpr/ppermute | solution.py:16
  155.1 4.2 %collective-permute-done = bf16[1,8,16,768]{3,2,1,0:T(8,128)(2,1)S(1)} collective-permute-done((bf16[1,8,16,768]{3,2,1,0:T(8,128)(2,1)S(1)}, bf16[1,8,16,768]{3,2,1,0:T(8,128)(2,1)S(1)}, u32[]{:S(2)}, u32[]{:S(2)}) %collective-permute-start) | collective-permute-done | bytes 196640 | tf_op jit(solution)/shard_map/while/body/eval_jaxpr/ppermute | solution.py:16
  159.3 10.2 %conditional.5 = (bf16[1,8,16,768]{3,2,1,0:T(8,128)(2,1)S(1)}) conditional(s32[]{:T(128)} %convert_element_type.176, () %tuple.160, (pred[]{:T(512)}, bf16[4,1,8,16,768]{4,3,2,1,0:T(8,128)(2,1)S(1)}, s32[]{:T(128)}, bf16[1,8,16,768]{3,2,1,0:T(8,128)(2,1)S(1)}, s32[4]{0:T(128)S(1)}, /*index=5*/bf16[768]{0:T(1024)(128)(2,1)S(1)}, ...), branch_computations={%region_5.5_spmd, %region_6.8_spmd} | conditional | flops 617591168 | bytes 9590903 | solution.py:72
  161.9 3.5 %fusion.242 = (f32[8,16]{1,0:T(8,128)S(1)}, f32[1,8,16,768]{3,2,1,0:T(8,128)S(1)}) fusion(f32[768]{0:T(1024)S(1)} %fusion.235, f32[768]{0:T(1024)S(1)} %convert_element_type.149, f32[768]{0:T(1024)S(1)} %get-tuple-element.768, f32[768]{0:T(1024)S(1)} %get-tuple-element.769, f32[768]{0:T(1024)S(1)} %get-tuple-element.770, f32[768]{0:T(1024)S(1)} %get-tuple-element.771, ...), kind=kLoop, calls=%fused_computation.461 | loop fusion | flops 9830272 | bytes 943616 | tf_op jit(solution)/shard_map/while/body/eval_jaxpr/cond/branch_1_fun/reduce_sum | solution.py:48
  165.8 3.7 %fusion.129 = f32[128,768]{1,0:T(8,128)S(1)} fusion(bf16[1536,768]{1,0:T(8,128)(2,1)} %get-tuple-element.690, f32[1536]{0:T(1024)S(1)} %fusion.234, bf16[128,768]{1,0:T(8,128)(2,1)S(1)} %bitcast.51, bf16[1536,768]{1,0:T(8,128)(2,1)} %get-tuple-element.689), kind=kOutput, calls=%fused_computation.285 | convolution fusion | flops 605945856 | bytes 5314560 | tf_op jit(solution)/shard_map/while/body/eval_jaxpr/cond/branch_1_fun/dot_general | solution.py:58
  169.6 1.5 collective-permute-start.1
  171.1 1.3 collective-permute-start
  172.6 2.2 collective-permute-done.1
  174.8 4.8 %collective-permute-done = bf16[1,8,16,768]{3,2,1,0:T(8,128)(2,1)S(1)} collective-permute-done((bf16[1,8,16,768]{3,2,1,0:T(8,128)(2,1)S(1)}, bf16[1,8,16,768]{3,2,1,0:T(8,128)(2,1)S(1)}, u32[]{:S(2)}, u32[]{:S(2)}) %collective-permute-start) | collective-permute-done | bytes 196640 | tf_op jit(solution)/shard_map/while/body/eval_jaxpr/ppermute | solution.py:16
  179.7 12.5 %collective-permute-start.1 = (bf16[1,8,16,768]{3,2,1,0:T(8,128)(2,1)S(1)}, bf16[1,8,16,768]{3,2,1,0:T(8,128)(2,1)S(1)}, u32[]{:S(2)}, u32[]{:S(2)}) collective-permute-start(bf16[1,8,16,768]{3,2,1,0:T(8,128)(2,1)S(1)} %get-tuple-element.1098), channel_id=1, source_target_pairs={{8,0},{16,8},{24,16},{9,1},{17,9},{25,17},{10,2},{18,10},{26,18},{... | collective-permute-start | bytes 589832 | tf_op jit(solution)/shard_map/while/body/eval_jaxpr/ppermute | solution.py:16
  192.3 1.3 collective-permute-start
  193.8 1.6 collective-permute-done.1
  195.4 12.6 %collective-permute-done = bf16[1,8,16,768]{3,2,1,0:T(8,128)(2,1)S(1)} collective-permute-done((bf16[1,8,16,768]{3,2,1,0:T(8,128)(2,1)S(1)}, bf16[1,8,16,768]{3,2,1,0:T(8,128)(2,1)S(1)}, u32[]{:S(2)}, u32[]{:S(2)}) %collective-permute-start) | collective-permute-done | bytes 196640 | tf_op jit(solution)/shard_map/while/body/eval_jaxpr/ppermute | solution.py:16
  208.0 4.8 %collective-permute-start.1 = (bf16[1,8,16,768]{3,2,1,0:T(8,128)(2,1)S(1)}, bf16[1,8,16,768]{3,2,1,0:T(8,128)(2,1)S(1)}, u32[]{:S(2)}, u32[]{:S(2)}) collective-permute-start(bf16[1,8,16,768]{3,2,1,0:T(8,128)(2,1)S(1)} %get-tuple-element.1098), channel_id=1, source_target_pairs={{8,0},{16,8},{24,16},{9,1},{17,9},{25,17},{10,2},{18,10},{26,18},{... | collective-permute-start | bytes 589832 | tf_op jit(solution)/shard_map/while/body/eval_jaxpr/ppermute | solution.py:16
  212.9 10.2 %conditional.4 = (bf16[1,8,16,768]{3,2,1,0:T(8,128)(2,1)S(1)}) conditional(s32[]{:T(128)} %convert_element_type.175, () %tuple.158, (pred[]{:T(512)}, bf16[4,1,8,16,768]{4,3,2,1,0:T(8,128)(2,1)S(1)}, s32[]{:T(128)}, bf16[1,8,16,768]{3,2,1,0:T(8,128)(2,1)S(1)}, s32[4]{0:T(128)S(1)}, /*index=5*/bf16[768]{0:T(1024)(128)(2,1)S(1)}, ...), branch_computations={%region_1.1_spmd, %region_2.4_spmd} | conditional | flops 617591168 | bytes 9590903 | solution.py:72
  215.4 3.5 %fusion.240 = (f32[8,16]{1,0:T(8,128)S(1)}, f32[1,8,16,768]{3,2,1,0:T(8,128)S(1)}) fusion(f32[768]{0:T(1024)S(1)} %fusion.115, f32[768]{0:T(1024)S(1)} %convert_element_type.137, f32[768]{0:T(1024)S(1)} %get-tuple-element.719, f32[768]{0:T(1024)S(1)} %get-tuple-element.720, f32[768]{0:T(1024)S(1)} %get-tuple-element.721, f32[768]{0:T(1024)S(1)} %get-tuple-element.722, ...), kind=kLoop, calls=%fused_computation.460 | loop fusion | flops 9830272 | bytes 943616 | tf_op jit(solution)/shard_map/while/body/eval_jaxpr/cond/branch_1_fun/reduce_sum | solution.py:48
  219.3 3.7 %fusion.9 = f32[128,768]{1,0:T(8,128)S(1)} fusion(bf16[1536,768]{1,0:T(8,128)(2,1)} %get-tuple-element.678, f32[1536]{0:T(1024)S(1)} %fusion.114, bf16[128,768]{1,0:T(8,128)(2,1)S(1)} %bitcast.52, bf16[1536,768]{1,0:T(8,128)(2,1)} %get-tuple-element.677), kind=kOutput, calls=%fused_computation.58 | convolution fusion | flops 605945856 | bytes 5314560 | tf_op jit(solution)/shard_map/while/body/eval_jaxpr/cond/branch_1_fun/dot_general | solution.py:58
  223.1 1.3 collective-permute-start
  224.6 13.8 %collective-permute-done = bf16[1,8,16,768]{3,2,1,0:T(8,128)(2,1)S(1)} collective-permute-done((bf16[1,8,16,768]{3,2,1,0:T(8,128)(2,1)S(1)}, bf16[1,8,16,768]{3,2,1,0:T(8,128)(2,1)S(1)}, u32[]{:S(2)}, u32[]{:S(2)}) %collective-permute-start) | collective-permute-done | bytes 196640 | tf_op jit(solution)/shard_map/while/body/eval_jaxpr/ppermute | solution.py:16
  238.4 6.0 %collective-permute-start.1 = (bf16[1,8,16,768]{3,2,1,0:T(8,128)(2,1)S(1)}, bf16[1,8,16,768]{3,2,1,0:T(8,128)(2,1)S(1)}, u32[]{:S(2)}, u32[]{:S(2)}) collective-permute-start(bf16[1,8,16,768]{3,2,1,0:T(8,128)(2,1)S(1)} %get-tuple-element.1098), channel_id=1, source_target_pairs={{8,0},{16,8},{24,16},{9,1},{17,9},{25,17},{10,2},{18,10},{26,18},{... | collective-permute-start | bytes 589832 | tf_op jit(solution)/shard_map/while/body/eval_jaxpr/ppermute | solution.py:16
  244.4 10.2 %conditional.4 = (bf16[1,8,16,768]{3,2,1,0:T(8,128)(2,1)S(1)}) conditional(s32[]{:T(128)} %convert_element_type.175, () %tuple.158, (pred[]{:T(512)}, bf16[4,1,8,16,768]{4,3,2,1,0:T(8,128)(2,1)S(1)}, s32[]{:T(128)}, bf16[1,8,16,768]{3,2,1,0:T(8,128)(2,1)S(1)}, s32[4]{0:T(128)S(1)}, /*index=5*/bf16[768]{0:T(1024)(128)(2,1)S(1)}, ...), branch_computations={%region_1.1_spmd, %region_2.4_spmd} | conditional | flops 617591168 | bytes 9590903 | solution.py:72
  246.9 3.5 %fusion.240 = (f32[8,16]{1,0:T(8,128)S(1)}, f32[1,8,16,768]{3,2,1,0:T(8,128)S(1)}) fusion(f32[768]{0:T(1024)S(1)} %fusion.115, f32[768]{0:T(1024)S(1)} %convert_element_type.137, f32[768]{0:T(1024)S(1)} %get-tuple-element.719, f32[768]{0:T(1024)S(1)} %get-tuple-element.720, f32[768]{0:T(1024)S(1)} %get-tuple-element.721, f32[768]{0:T(1024)S(1)} %get-tuple-element.722, ...), kind=kLoop, calls=%fused_computation.460 | loop fusion | flops 9830272 | bytes 943616 | tf_op jit(solution)/shard_map/while/body/eval_jaxpr/cond/branch_1_fun/reduce_sum | solution.py:48
  250.9 3.7 %fusion.9 = f32[128,768]{1,0:T(8,128)S(1)} fusion(bf16[1536,768]{1,0:T(8,128)(2,1)} %get-tuple-element.678, f32[1536]{0:T(1024)S(1)} %fusion.114, bf16[128,768]{1,0:T(8,128)(2,1)S(1)} %bitcast.52, bf16[1536,768]{1,0:T(8,128)(2,1)} %get-tuple-element.677), kind=kOutput, calls=%fused_computation.58 | convolution fusion | flops 605945856 | bytes 5314560 | tf_op jit(solution)/shard_map/while/body/eval_jaxpr/cond/branch_1_fun/dot_general | solution.py:58
  254.6 1.3 collective-permute-start
  256.1 6.1 %collective-permute-done = bf16[1,8,16,768]{3,2,1,0:T(8,128)(2,1)S(1)} collective-permute-done((bf16[1,8,16,768]{3,2,1,0:T(8,128)(2,1)S(1)}, bf16[1,8,16,768]{3,2,1,0:T(8,128)(2,1)S(1)}, u32[]{:S(2)}, u32[]{:S(2)}) %collective-permute-start) | collective-permute-done | bytes 196640 | tf_op jit(solution)/shard_map/while/body/eval_jaxpr/ppermute | solution.py:16
  262.2 0.9 copy-done
  (148 shorter events, 16.7 us)
Async XLA Ops:
  6.5 132.2 %copy-start.2 = (bf16[1,7,7,768]{3,2,1,0:T(8,128)(2,1)S(1)}, bf16[1,7,7,768]{3,2,1,0:T(8,128)(2,1)}, u32[]{:S(2)}) copy-start(bf16[1,7,7,768]{3,2,1,0:T(8,128)(2,1)} %param.17) | copy-start | bytes 225796
  6.5 132.2 %copy-start.1 = (bf16[4,1,8,16,768]{4,3,2,1,0:T(8,128)(2,1)S(1)}, bf16[4,1,8,16,768]{4,3,2,1,0:T(8,128)(2,1)}, u32[]{:S(2)}) copy-start(bf16[4,1,8,16,768]{4,3,2,1,0:T(8,128)(2,1)} %param.15) | copy-start | bytes 2359300
  6.5 132.2 %copy-start.5 = (s32[4]{0:T(128)S(1)}, s32[4]{0:T(128)}, u32[]{:S(2)}) copy-start(s32[4]{0:T(128)} %param.16) | copy-start | bytes 52
  6.5 50.7 %all-gather.5.cloned.1.call-start = ((), (), s32[]{:S(2)}) async-start(), calls=%async_computation | async-start | bytes 2654208 | tf_op jit(solution)/shard_map/all_gather | solution.py:101
  7.3 66.7 %all-gather.7.cloned.1.call-start = ((), (), s32[]{:S(2)}) async-start(), calls=%async_computation.1 | async-start | bytes 2654208 | tf_op jit(solution)/shard_map/all_gather | solution.py:102
  8.0 98.4 %all-gather.9.cloned.1.call-start = ((), (), s32[]{:S(2)}) async-start(), calls=%async_computation.2 | async-start | bytes 2654208 | tf_op jit(solution)/shard_map/all_gather | solution.py:103
  8.1 9.0 %collective-permute-start.12 = (bf16[1,192,768]{2,1,0:T(8,128)(2,1)}, bf16[1,192,768]{2,1,0:T(8,128)(2,1)S(1)}, u32[]{:S(2)}, u32[]{:S(2)}) collective-permute-start(bf16[1,192,768]{2,1,0:T(8,128)(2,1)} %param.21), channel_id=1, source_target_pairs={{0,8},{8,0},{16,24},{24,16},{1,9},{9,1},{17,25},{25,17},{2,10},{10... | collective-permute-start | bytes 884744 | tf_op jit(solution)/shard_map/ppermute | solution.py:10
  17.1 7.9 %collective-permute-start.13 = (bf16[1,192,768]{2,1,0:T(8,128)(2,1)S(1)}, bf16[1,192,768]{2,1,0:T(8,128)(2,1)S(1)}, u32[]{:S(2)}, u32[]{:S(2)}) collective-permute-start(bf16[1,192,768]{2,1,0:T(8,128)(2,1)S(1)} %collective-permute-done.12), channel_id=1, source_target_pairs={{0,16},{8,24},{16,0},{24,8},{1,17},{9,25},{17,1},{25,9},{2,18},{10... | collective-permute-start | bytes 884744 | tf_op jit(solution)/shard_map/ppermute | solution.py:10
  25.0 0.7 copy-start.3
  25.7 112.9 %all-gather.11.cloned.1.call-start = ((), (), s32[]{:S(2)}) async-start(), calls=%async_computation.3 | async-start | bytes 2654208 | tf_op jit(solution)/shard_map/all_gather | solution.py:104
  25.8 7.4 %collective-permute-start.14 = (bf16[1,192,768]{2,1,0:T(8,128)(2,1)}, bf16[1,192,768]{2,1,0:T(8,128)(2,1)S(1)}, u32[]{:S(2)}, u32[]{:S(2)}) collective-permute-start(bf16[1,192,768]{2,1,0:T(8,128)(2,1)} %param.22), channel_id=1, source_target_pairs={{0,8},{8,0},{16,24},{24,16},{1,9},{9,1},{17,25},{25,17},{2,10},{10... | collective-permute-start | bytes 884744 | tf_op jit(solution)/shard_map/ppermute | solution.py:10
  33.2 6.7 %collective-permute-start.15 = (bf16[1,192,768]{2,1,0:T(8,128)(2,1)S(1)}, bf16[1,192,768]{2,1,0:T(8,128)(2,1)S(1)}, u32[]{:S(2)}, u32[]{:S(2)}) collective-permute-start(bf16[1,192,768]{2,1,0:T(8,128)(2,1)S(1)} %collective-permute-done.14), channel_id=1, source_target_pairs={{0,16},{8,24},{16,0},{24,8},{1,17},{9,25},{17,1},{25,9},{2,18},{10... | collective-permute-start | bytes 884744 | tf_op jit(solution)/shard_map/ppermute | solution.py:10
  39.9 0.7 copy-start.4
  40.6 4.8 %collective-permute-start.4 = (bf16[1,7,7,768]{3,2,1,0:T(8,128)(2,1)}, bf16[1,7,7,768]{3,2,1,0:T(8,128)(2,1)S(1)}, u32[]{:S(2)}, u32[]{:S(2)}) collective-permute-start(bf16[1,7,7,768]{3,2,1,0:T(8,128)(2,1)} %param.17), channel_id=1, source_target_pairs={{0,8},{8,0},{16,24},{24,16},{1,9},{9,1},{17,25},{25,17},{2,10},{10... | collective-permute-start | bytes 225800 | tf_op jit(solution)/shard_map/ppermute | solution.py:10
  45.4 11.7 %collective-permute-start.5 = (bf16[1,7,7,768]{3,2,1,0:T(8,128)(2,1)S(1)}, bf16[1,7,7,768]{3,2,1,0:T(8,128)(2,1)S(1)}, u32[]{:S(2)}, u32[]{:S(2)}) collective-permute-start(bf16[1,7,7,768]{3,2,1,0:T(8,128)(2,1)S(1)} %collective-permute-done.4), channel_id=1, source_target_pairs={{0,16},{8,24},{16,0},{24,8},{1,17},{9,25},{17,1},{25,9},{2,18},{10... | collective-permute-start | bytes 225800 | tf_op jit(solution)/shard_map/ppermute | solution.py:10
  46.0 4.1 %collective-permute-start.2 = (bf16[1,768]{1,0:T(2,128)(2,1)}, bf16[1,768]{1,0:T(2,128)(2,1)S(1)}, u32[]{:S(2)}, u32[]{:S(2)}) collective-permute-start(bf16[1,768]{1,0:T(2,128)(2,1)} %param.23), channel_id=1, source_target_pairs={{0,8},{8,0},{16,24},{24,16},{1,9},{9,1},{17,25},{25,17},{2,10},{10... | collective-permute-start | bytes 4616 | tf_op jit(solution)/shard_map/ppermute | solution.py:10
  46.8 4.7 %collective-permute-start.6 = (bf16[1,768]{1,0:T(2,128)(2,1)}, bf16[1,768]{1,0:T(2,128)(2,1)S(1)}, u32[]{:S(2)}, u32[]{:S(2)}) collective-permute-start(bf16[1,768]{1,0:T(2,128)(2,1)} %param.18), channel_id=1, source_target_pairs={{0,8},{8,0},{16,24},{24,16},{1,9},{9,1},{17,25},{25,17},{2,10},{10... | collective-permute-start | bytes 4616 | tf_op jit(solution)/shard_map/ppermute | solution.py:10
  48.0 4.1 %collective-permute-start.8 = (bf16[1,768]{1,0:T(2,128)(2,1)}, bf16[1,768]{1,0:T(2,128)(2,1)S(1)}, u32[]{:S(2)}, u32[]{:S(2)}) collective-permute-start(bf16[1,768]{1,0:T(2,128)(2,1)} %param.19), channel_id=1, source_target_pairs={{0,8},{8,0},{16,24},{24,16},{1,9},{9,1},{17,25},{25,17},{2,10},{10... | collective-permute-start | bytes 4616 | tf_op jit(solution)/shard_map/ppermute | solution.py:10
  48.8 4.7 %collective-permute-start.10 = (bf16[1,768]{1,0:T(2,128)(2,1)}, bf16[1,768]{1,0:T(2,128)(2,1)S(1)}, u32[]{:S(2)}, u32[]{:S(2)}) collective-permute-start(bf16[1,768]{1,0:T(2,128)(2,1)} %param.20), channel_id=1, source_target_pairs={{0,8},{8,0},{16,24},{24,16},{1,9},{9,1},{17,25},{25,17},{2,10},{10... | collective-permute-start | bytes 4616 | tf_op jit(solution)/shard_map/ppermute | solution.py:10
  50.0 6.9 %collective-permute-start.3 = (bf16[1,768]{1,0:T(2,128)(2,1)S(1)}, bf16[1,768]{1,0:T(2,128)(2,1)S(1)}, u32[]{:S(2)}, u32[]{:S(2)}) collective-permute-start(bf16[1,768]{1,0:T(2,128)(2,1)S(1)} %collective-permute-done.2), channel_id=1, source_target_pairs={{0,16},{8,24},{16,0},{24,8},{1,17},{9,25},{17,1},{25,9},{2,18},{10... | collective-permute-start | bytes 4616 | tf_op jit(solution)/shard_map/ppermute | solution.py:10
  51.5 5.4 %collective-permute-start.7 = (bf16[1,768]{1,0:T(2,128)(2,1)S(1)}, bf16[1,768]{1,0:T(2,128)(2,1)S(1)}, u32[]{:S(2)}, u32[]{:S(2)}) collective-permute-start(bf16[1,768]{1,0:T(2,128)(2,1)S(1)} %collective-permute-done.6), channel_id=1, source_target_pairs={{0,16},{8,24},{16,0},{24,8},{1,17},{9,25},{17,1},{25,9},{2,18},{10... | collective-permute-start | bytes 4616 | tf_op jit(solution)/shard_map/ppermute | solution.py:10
  52.1 4.9 %collective-permute-start.9 = (bf16[1,768]{1,0:T(2,128)(2,1)S(1)}, bf16[1,768]{1,0:T(2,128)(2,1)S(1)}, u32[]{:S(2)}, u32[]{:S(2)}) collective-permute-start(bf16[1,768]{1,0:T(2,128)(2,1)S(1)} %collective-permute-done.8), channel_id=1, source_target_pairs={{0,16},{8,24},{16,0},{24,8},{1,17},{9,25},{17,1},{25,9},{2,18},{10... | collective-permute-start | bytes 4616 | tf_op jit(solution)/shard_map/ppermute | solution.py:10
  53.6 3.6 %collective-permute-start.11 = (bf16[1,768]{1,0:T(2,128)(2,1)S(1)}, bf16[1,768]{1,0:T(2,128)(2,1)S(1)}, u32[]{:S(2)}, u32[]{:S(2)}) collective-permute-start(bf16[1,768]{1,0:T(2,128)(2,1)S(1)} %collective-permute-done.10), channel_id=1, source_target_pairs={{0,16},{8,24},{16,0},{24,8},{1,17},{9,25},{17,1},{25,9},{2,18},{10... | collective-permute-start | bytes 4616 | tf_op jit(solution)/shard_map/ppermute | solution.py:10
  149.0 6.1 %collective-permute-start.1 = (bf16[1,8,16,768]{3,2,1,0:T(8,128)(2,1)S(1)}, bf16[1,8,16,768]{3,2,1,0:T(8,128)(2,1)S(1)}, u32[]{:S(2)}, u32[]{:S(2)}) collective-permute-start(bf16[1,8,16,768]{3,2,1,0:T(8,128)(2,1)S(1)} %get-tuple-element.1098), channel_id=1, source_target_pairs={{8,0},{16,8},{24,16},{9,1},{17,9},{25,17},{10,2},{18,10},{26,18},{... | collective-permute-start | bytes 589832 | tf_op jit(solution)/shard_map/while/body/eval_jaxpr/ppermute | solution.py:16
  150.4 8.9 %collective-permute-start = (bf16[1,8,16,768]{3,2,1,0:T(8,128)(2,1)S(1)}, bf16[1,8,16,768]{3,2,1,0:T(8,128)(2,1)S(1)}, u32[]{:S(2)}, u32[]{:S(2)}) collective-permute-start(bf16[1,8,16,768]{3,2,1,0:T(8,128)(2,1)S(1)} %get-tuple-element.1097), channel_id=1, source_target_pairs={{0,8},{8,16},{16,24},{1,9},{9,17},{17,25},{2,10},{10,18},{18,26},{... | collective-permute-start | bytes 589832 | tf_op jit(solution)/shard_map/while/body/eval_jaxpr/ppermute | solution.py:16
  169.6 5.3 %collective-permute-start.1 = (bf16[1,8,16,768]{3,2,1,0:T(8,128)(2,1)S(1)}, bf16[1,8,16,768]{3,2,1,0:T(8,128)(2,1)S(1)}, u32[]{:S(2)}, u32[]{:S(2)}) collective-permute-start(bf16[1,8,16,768]{3,2,1,0:T(8,128)(2,1)S(1)} %get-tuple-element.1098), channel_id=1, source_target_pairs={{8,0},{16,8},{24,16},{9,1},{17,9},{25,17},{10,2},{18,10},{26,18},{... | collective-permute-start | bytes 589832 | tf_op jit(solution)/shard_map/while/body/eval_jaxpr/ppermute | solution.py:16
  171.1 8.6 %collective-permute-start = (bf16[1,8,16,768]{3,2,1,0:T(8,128)(2,1)S(1)}, bf16[1,8,16,768]{3,2,1,0:T(8,128)(2,1)S(1)}, u32[]{:S(2)}, u32[]{:S(2)}) collective-permute-start(bf16[1,8,16,768]{3,2,1,0:T(8,128)(2,1)S(1)} %get-tuple-element.1097), channel_id=1, source_target_pairs={{0,8},{8,16},{16,24},{1,9},{9,17},{17,25},{2,10},{10,18},{18,26},{... | collective-permute-start | bytes 589832 | tf_op jit(solution)/shard_map/while/body/eval_jaxpr/ppermute | solution.py:16
  179.7 15.7 %collective-permute-start.1 = (bf16[1,8,16,768]{3,2,1,0:T(8,128)(2,1)S(1)}, bf16[1,8,16,768]{3,2,1,0:T(8,128)(2,1)S(1)}, u32[]{:S(2)}, u32[]{:S(2)}) collective-permute-start(bf16[1,8,16,768]{3,2,1,0:T(8,128)(2,1)S(1)} %get-tuple-element.1098), channel_id=1, source_target_pairs={{8,0},{16,8},{24,16},{9,1},{17,9},{25,17},{10,2},{18,10},{26,18},{... | collective-permute-start | bytes 589832 | tf_op jit(solution)/shard_map/while/body/eval_jaxpr/ppermute | solution.py:16
  192.3 15.7 %collective-permute-start = (bf16[1,8,16,768]{3,2,1,0:T(8,128)(2,1)S(1)}, bf16[1,8,16,768]{3,2,1,0:T(8,128)(2,1)S(1)}, u32[]{:S(2)}, u32[]{:S(2)}) collective-permute-start(bf16[1,8,16,768]{3,2,1,0:T(8,128)(2,1)S(1)} %get-tuple-element.1097), channel_id=1, source_target_pairs={{0,8},{8,16},{16,24},{1,9},{9,17},{17,25},{2,10},{10,18},{18,26},{... | collective-permute-start | bytes 589832 | tf_op jit(solution)/shard_map/while/body/eval_jaxpr/ppermute | solution.py:16
  208.0 16.5 %collective-permute-start.1 = (bf16[1,8,16,768]{3,2,1,0:T(8,128)(2,1)S(1)}, bf16[1,8,16,768]{3,2,1,0:T(8,128)(2,1)S(1)}, u32[]{:S(2)}, u32[]{:S(2)}) collective-permute-start(bf16[1,8,16,768]{3,2,1,0:T(8,128)(2,1)S(1)} %get-tuple-element.1098), channel_id=1, source_target_pairs={{8,0},{16,8},{24,16},{9,1},{17,9},{25,17},{10,2},{18,10},{26,18},{... | collective-permute-start | bytes 589832 | tf_op jit(solution)/shard_map/while/body/eval_jaxpr/ppermute | solution.py:16
  223.1 15.3 %collective-permute-start = (bf16[1,8,16,768]{3,2,1,0:T(8,128)(2,1)S(1)}, bf16[1,8,16,768]{3,2,1,0:T(8,128)(2,1)S(1)}, u32[]{:S(2)}, u32[]{:S(2)}) collective-permute-start(bf16[1,8,16,768]{3,2,1,0:T(8,128)(2,1)S(1)} %get-tuple-element.1097), channel_id=1, source_target_pairs={{0,8},{8,16},{16,24},{1,9},{9,17},{17,25},{2,10},{10,18},{18,26},{... | collective-permute-start | bytes 589832 | tf_op jit(solution)/shard_map/while/body/eval_jaxpr/ppermute | solution.py:16
  238.4 17.7 %collective-permute-start.1 = (bf16[1,8,16,768]{3,2,1,0:T(8,128)(2,1)S(1)}, bf16[1,8,16,768]{3,2,1,0:T(8,128)(2,1)S(1)}, u32[]{:S(2)}, u32[]{:S(2)}) collective-permute-start(bf16[1,8,16,768]{3,2,1,0:T(8,128)(2,1)S(1)} %get-tuple-element.1098), channel_id=1, source_target_pairs={{8,0},{16,8},{24,16},{9,1},{17,9},{25,17},{10,2},{18,10},{26,18},{... | collective-permute-start | bytes 589832 | tf_op jit(solution)/shard_map/while/body/eval_jaxpr/ppermute | solution.py:16
  254.6 7.6 %collective-permute-start = (bf16[1,8,16,768]{3,2,1,0:T(8,128)(2,1)S(1)}, bf16[1,8,16,768]{3,2,1,0:T(8,128)(2,1)S(1)}, u32[]{:S(2)}, u32[]{:S(2)}) collective-permute-start(bf16[1,8,16,768]{3,2,1,0:T(8,128)(2,1)S(1)} %get-tuple-element.1097), channel_id=1, source_target_pairs={{0,8},{8,16},{16,24},{1,9},{9,17},{17,25},{2,10},{10,18},{18,26},{... | collective-permute-start | bytes 589832 | tf_op jit(solution)/shard_map/while/body/eval_jaxpr/ppermute | solution.py:16
  262.2 0.9 copy-start
Sparse Core Ops, SparseCore 0:
  9.0 32.6 all-gather.4
  43.3 30.6 all-gather.6
  75.6 30.6 all-gather.8
  107.9 30.6 all-gather.10
where the time goes:
time: 270 us
  waiting for transfers between devices  165 us (61%)
  starting transfers between devices  44.2 us (16%)
  other arithmetic  19.5 us (7%)
  matrix products  14.7 us (5%)
  between operations  13.2 us (5%)
  local copies, waits for them, and re-layouts  7.06 us (3%)
  loops' own time  6.28 us (2%)
    ppermute x10, waiting for transfers between devices, passed_along(): lax.ppermute(value, axis, [(source, source + steps) for source in range(i...  48.6 us
    ppermute x14, waiting for transfers between devices, swapped(): return lax.ppermute(value, axis, pairs)  33.2 us
    ppermute x10, starting transfers between devices, passed_along(): lax.ppermute(value, axis, [(source, source + steps) for source in range(i...  32.6 us
    all_gather x1, waiting for transfers between devices, on_device(): lax.all_gather(shards[0], 'dp', axis=1, tiled=True)  32.4 us
    all_gather x1, waiting for transfers between devices, on_device(): lax.all_gather(shards[1], 'dp', axis=1, tiled=True)  32.2 us
    all_gather x1, waiting for transfers between devices, on_device(): lax.all_gather(w_out, 'dp', axis=1, tiled=True)  16.8 us
    dot_general x4, matrix products, conv_block(): jnp.dot(activated, w_out, preferred_element_type=jnp.float32)  14.7 us
    reduce_sum x4, other arithmetic, conv_block(): average = jnp.sum(spatial, axis=-1, keepdims=True) / channel_count  13.8 us
  transfers between devices with their start and end apart: 28, of which 17 were waited for; matrix products, arithmetic and copies ran while one was open for 8% of the time, Pallas kernels for 0%

commit v1 on v0

--- a/solution.py
+++ b/solution.py
@@ -2,6 +2,18 @@
 import jax.numpy as jnp
 from jax import lax
 from jax.sharding import PartitionSpec as P
+
+
+def collect(array, axis, dim):
+    ways, here = (lax.axis_size(axis), lax.axis_index(axis))
+    grown, reach = (array, 1)
+    while reach < ways:
+        theirs = lax.ppermute(grown, axis, [(d, d ^ reach) for d in range(ways)])
+        mine_first = jnp.concatenate([grown, theirs], axis=dim)
+        theirs_first = jnp.concatenate([theirs, grown], axis=dim)
+        grown = jnp.where(here & reach == 0, mine_first, theirs_first)
+        reach = 2 * reach
+    return grown
 
 
 def swapped(value, axis, stride):
@@ -100,7 +112,7 @@
     full_in, full_out, mirror_in, mirror_out = (
         lax.all_gather(w_in, "dp", axis=1, tiled=True),
         lax.all_gather(w_out, "dp", axis=1, tiled=True),
-        lax.all_gather(shards[0], "dp", axis=1, tiled=True),
+        collect(shards[0], "dp", 1),
         lax.all_gather(shards[1], "dp", axis=1, tiled=True),
     )
     own_params = (

time: 270 us -> 279 us (1.033)
  starting transfers between devices: 44.2 us -> 52.8 us
    ppermute x0 -> x3, waiting for transfers between devices: none -> 82.6 us  [collect(): theirs = lax.ppermute(grown, axis, [(d, d ^ reach) for d in range(ways)])]
    all_gather x1 -> x0, waiting for transfers between devices: 32.4 us -> none  [on_device(): lax.all_gather(shards[0], 'dp', axis=1, tiled=True)]
    all_gather x1, waiting for transfers between devices: 32.2 us -> 0.01 us  [on_device(): lax.all_gather(shards[1], 'dp', axis=1, tiled=True)]
    all_gather x1, waiting for transfers between devices: 16.8 us -> 0.01 us  [on_device(): lax.all_gather(w_out, 'dp', axis=1, tiled=True)]
    ppermute x0 -> x3, starting transfers between devices: none -> 7.37 us  [collect(): theirs = lax.ppermute(grown, axis, [(d, d ^ reach) for d in range(ways)])]
    select_n x0 -> x5, other arithmetic: none -> 4.09 us  [collect(): grown = jnp.where(here & reach == 0, mine_first, theirs_first)]
  transfers between devices with their start and end apart: 28 -> 30, of which waited for: 17 -> 20; matrix products, arithmetic and copies ran while one was open for 8% -> 8% of each run, Pallas kernels for 0% -> 0%
where the time goes in v1:
time: 279 us; the launch traced here: 278 us
  waiting for transfers between devices  164 us (59%)
  starting transfers between devices  52.8 us (19%)
  other arithmetic  20.8 us (7%)
  matrix products  14.7 us (5%)
  between operations  13.2 us (5%)
  loops' own time  6.3 us (2%)
  local copies, waits for them, and re-layouts  6.26 us (2%)
    ppermute x3, waiting for transfers between devices, collect(): theirs = lax.ppermute(grown, axis, [(d, d ^ reach) for d in range(ways)])  82.6 us
    ppermute x10, waiting for transfers between devices, passed_along(): lax.ppermute(value, axis, [(source, source + steps) for source in range(i...  47 us
    ppermute x10, starting transfers between devices, passed_along(): lax.ppermute(value, axis, [(source, source + steps) for source in range(i...  33.6 us
    ppermute x14, waiting for transfers between devices, swapped(): return lax.ppermute(value, axis, pairs)  33 us
    dot_general x4, matrix products, conv_block(): jnp.dot(activated, w_out, preferred_element_type=jnp.float32)  14.7 us
    reduce_sum x4, other arithmetic, conv_block(): average = jnp.sum(spatial, axis=-1, keepdims=True) / channel_count  13.8 us
    ppermute x14, starting transfers between devices, swapped(): return lax.ppermute(value, axis, pairs)  11.7 us
    ppermute x3, starting transfers between devices, collect(): theirs = lax.ppermute(grown, axis, [(d, d ^ reach) for d in range(ways)])  7.37 us
  transfers between devices with their start and end apart: 30, of which 20 were waited for; matrix products, arithmetic and copies ran while one was open for 8% of the time, Pallas kernels for 0%

profile of v1, /device:TPU:6, one launch (start us, length us, event | category | flops | bytes accessed | tf_op | source)
XLA Modules:
  0.0 278.1 jit_solution(16417299209188390887)
XLA Ops:
  8.7 8.4 %collective-permute-done.17 = bf16[1,192,768]{2,1,0:T(8,128)(2,1)S(1)} collective-permute-done((bf16[1,192,768]{2,1,0:T(8,128)(2,1)}, bf16[1,192,768]{2,1,0:T(8,128)(2,1)S(1)}, u32[]{:S(2)}, u32[]{:S(2)}) %collective-permute-start.17) | collective-permute-done | bytes 294944 | tf_op jit(solution)/shard_map/ppermute | solution.py:22
  17.6 7.4 %collective-permute-done.18 = bf16[1,192,768]{2,1,0:T(8,128)(2,1)S(1)} collective-permute-done((bf16[1,192,768]{2,1,0:T(8,128)(2,1)S(1)}, bf16[1,192,768]{2,1,0:T(8,128)(2,1)S(1)}, u32[]{:S(2)}, u32[]{:S(2)}) %collective-permute-start.18) | collective-permute-done | bytes 294944 | tf_op jit(solution)/shard_map/ppermute | solution.py:22
  26.3 6.8 %collective-permute-done.12 = bf16[1,192,768]{2,1,0:T(8,128)(2,1)S(1)} collective-permute-done((bf16[1,192,768]{2,1,0:T(8,128)(2,1)}, bf16[1,192,768]{2,1,0:T(8,128)(2,1)S(1)}, u32[]{:S(2)}, u32[]{:S(2)}) %collective-permute-start.12) | collective-permute-done | bytes 294944 | tf_op jit(solution)/shard_map/ppermute | solution.py:22
  33.6 6.2 %collective-permute-done.13 = bf16[1,192,768]{2,1,0:T(8,128)(2,1)S(1)} collective-permute-done((bf16[1,192,768]{2,1,0:T(8,128)(2,1)S(1)}, bf16[1,192,768]{2,1,0:T(8,128)(2,1)S(1)}, u32[]{:S(2)}, u32[]{:S(2)}) %collective-permute-start.13) | collective-permute-done | bytes 294944 | tf_op jit(solution)/shard_map/ppermute | solution.py:22
  39.9 1.5 collective-permute-done.14
  41.6 1.6 collective-permute-start.15
  43.4 24.3 %collective-permute-done.15 = bf16[1,384,768]{2,1,0:T(8,128)(2,1)S(1)} collective-permute-done((bf16[1,384,768]{2,1,0:T(8,128)(2,1)S(1)}, bf16[1,384,768]{2,1,0:T(8,128)(2,1)S(1)}, u32[]{:S(2)}, u32[]{:S(2)}) %collective-permute-start.15) | collective-permute-done | bytes 589856 | tf_op jit(solution)/shard_map/ppermute | solution.py:11
  67.7 1.5 maximum_select_fusion.2
  69.2 5.7 %collective-permute-start.16 = (bf16[1,768,768]{2,1,0:T(8,128)(2,1)}, bf16[1,768,768]{2,1,0:T(8,128)(2,1)S(1)}, u32[]{:S(2)}, u32[]{:S(2)}) collective-permute-start(bf16[1,768,768]{2,1,0:T(8,128)(2,1)} %maximum_select_fusion.2), channel_id=1, source_target_pairs={{0,4},{1,5},{2,6},{3,7},{4,0},{5,1},{6,2},{7,3},{8,12},{9,13},{10,... | collective-permute-start | bytes 3538952 | tf_op jit(solution)/shard_map/ppermute | solution.py:11
  75.4 1.5 collective-permute-start.2
  77.5 1.5 collective-permute-start.8
  79.4 1.1 collective-permute-start.10
  81.1 1.5 collective-permute-start.7
  85.2 1.4 collective-permute-done.9
  86.7 1.1 collective-permute-done.11
  89.2 56.8 %collective-permute-done.16 = bf16[1,768,768]{2,1,0:T(8,128)(2,1)S(1)} collective-permute-done((bf16[1,768,768]{2,1,0:T(8,128)(2,1)}, bf16[1,768,768]{2,1,0:T(8,128)(2,1)S(1)}, u32[]{:S(2)}, u32[]{:S(2)}) %collective-permute-start.16) | collective-permute-done | bytes 1179680 | tf_op jit(solution)/shard_map/ppermute | solution.py:11
  146.0 1.8 maximum_select_fusion
  148.0 122.7 %while.19 = (s32[]{:T(128)}, bf16[1,8,16,768]{3,2,1,0:T(8,128)(2,1)S(1)}, bf16[1,8,16,768]{3,2,1,0:T(8,128)(2,1)S(1)}, bf16[4,1,8,16,768]{4,3,2,1,0:T(8,128)(2,1...) while((s32[]{:T(128)}, ...), condition=%wide.region_9.10_spmd, body=%wide.region_0.9_spmd.sunk | while | flops 1235378944 | bytes 22721452 | solution.py:168
  148.0 10.1 %conditional.5 = (bf16[1,8,16,768]{3,2,1,0:T(8,128)(2,1)S(1)}) conditional(s32[]{:T(128)} %convert_element_type.176, () %tuple.160, (pred[]{:T(512)}, bf16[4,1,8,16,768]{4,3,2,1,0:T(8,128)(2,1)S(1)}, s32[]{:T(128)}, bf16[1,8,16,768]{3,2,1,0:T(8,128)(2,1)S(1)}, s32[4]{0:T(128)S(1)}, /*index=5*/bf16[768]{0:T(1024)(128)(2,1)S(1)}, ...), branch_computations={%region_5.5_spmd, %region_6.8_spmd} | conditional | flops 617591168 | bytes 9590903 | solution.py:84
  150.4 3.5 %fusion.242 = (f32[8,16]{1,0:T(8,128)S(1)}, f32[1,8,16,768]{3,2,1,0:T(8,128)S(1)}) fusion(f32[768]{0:T(1024)S(1)} %fusion.235, f32[768]{0:T(1024)S(1)} %convert_element_type.149, f32[768]{0:T(1024)S(1)} %get-tuple-element.768, f32[768]{0:T(1024)S(1)} %get-tuple-element.769, f32[768]{0:T(1024)S(1)} %get-tuple-element.770, f32[768]{0:T(1024)S(1)} %get-tuple-element.771, ...), kind=kLoop, calls=%fused_computation.466 | loop fusion | flops 9830272 | bytes 943616 | tf_op jit(solution)/shard_map/while/body/eval_jaxpr/cond/branch_1_fun/reduce_sum | solution.py:60
  154.4 3.7 %fusion.129 = f32[128,768]{1,0:T(8,128)S(1)} fusion(bf16[1536,768]{1,0:T(8,128)(2,1)} %get-tuple-element.690, f32[1536]{0:T(1024)S(1)} %fusion.234, bf16[128,768]{1,0:T(8,128)(2,1)S(1)} %bitcast.56, bf16[1536,768]{1,0:T(8,128)(2,1)} %get-tuple-element.689), kind=kOutput, calls=%fused_computation.285 | convolution fusion | flops 605945856 | bytes 5314560 | tf_op jit(solution)/shard_map/while/body/eval_jaxpr/cond/branch_1_fun/dot_general | solution.py:70
  158.1 1.3 collective-permute-start.1
  159.5 1.3 collective-permute-start
  161.0 2.3 collective-permute-done.1
  163.3 4.2 %collective-permute-done = bf16[1,8,16,768]{3,2,1,0:T(8,128)(2,1)S(1)} collective-permute-done((bf16[1,8,16,768]{3,2,1,0:T(8,128)(2,1)S(1)}, bf16[1,8,16,768]{3,2,1,0:T(8,128)(2,1)S(1)}, u32[]{:S(2)}, u32[]{:S(2)}) %collective-permute-start) | collective-permute-done | bytes 196640 | tf_op jit(solution)/shard_map/while/body/eval_jaxpr/ppermute | solution.py:28
  167.5 10.1 %conditional.5 = (bf16[1,8,16,768]{3,2,1,0:T(8,128)(2,1)S(1)}) conditional(s32[]{:T(128)} %convert_element_type.176, () %tuple.160, (pred[]{:T(512)}, bf16[4,1,8,16,768]{4,3,2,1,0:T(8,128)(2,1)S(1)}, s32[]{:T(128)}, bf16[1,8,16,768]{3,2,1,0:T(8,128)(2,1)S(1)}, s32[4]{0:T(128)S(1)}, /*index=5*/bf16[768]{0:T(1024)(128)(2,1)S(1)}, ...), branch_computations={%region_5.5_spmd, %region_6.8_spmd} | conditional | flops 617591168 | bytes 9590903 | solution.py:84
  169.9 3.5 %fusion.242 = (f32[8,16]{1,0:T(8,128)S(1)}, f32[1,8,16,768]{3,2,1,0:T(8,128)S(1)}) fusion(f32[768]{0:T(1024)S(1)} %fusion.235, f32[768]{0:T(1024)S(1)} %convert_element_type.149, f32[768]{0:T(1024)S(1)} %get-tuple-element.768, f32[768]{0:T(1024)S(1)} %get-tuple-element.769, f32[768]{0:T(1024)S(1)} %get-tuple-element.770, f32[768]{0:T(1024)S(1)} %get-tuple-element.771, ...), kind=kLoop, calls=%fused_computation.466 | loop fusion | flops 9830272 | bytes 943616 | tf_op jit(solution)/shard_map/while/body/eval_jaxpr/cond/branch_1_fun/reduce_sum | solution.py:60
  173.8 3.7 %fusion.129 = f32[128,768]{1,0:T(8,128)S(1)} fusion(bf16[1536,768]{1,0:T(8,128)(2,1)} %get-tuple-element.690, f32[1536]{0:T(1024)S(1)} %fusion.234, bf16[128,768]{1,0:T(8,128)(2,1)S(1)} %bitcast.56, bf16[1536,768]{1,0:T(8,128)(2,1)} %get-tuple-element.689), kind=kOutput, calls=%fused_computation.285 | convolution fusion | flops 605945856 | bytes 5314560 | tf_op jit(solution)/shard_map/while/body/eval_jaxpr/cond/branch_1_fun/dot_general | solution.py:70
  177.5 1.5 collective-permute-start.1
  179.1 1.3 collective-permute-start
  180.5 1.6 collective-permute-done.1
  182.2 4.7 %collective-permute-done = bf16[1,8,16,768]{3,2,1,0:T(8,128)(2,1)S(1)} collective-permute-done((bf16[1,8,16,768]{3,2,1,0:T(8,128)(2,1)S(1)}, bf16[1,8,16,768]{3,2,1,0:T(8,128)(2,1)S(1)}, u32[]{:S(2)}, u32[]{:S(2)}) %collective-permute-start) | collective-permute-done | bytes 196640 | tf_op jit(solution)/shard_map/while/body/eval_jaxpr/ppermute | solution.py:28
  186.9 12.7 %collective-permute-start.1 = (bf16[1,8,16,768]{3,2,1,0:T(8,128)(2,1)S(1)}, bf16[1,8,16,768]{3,2,1,0:T(8,128)(2,1)S(1)}, u32[]{:S(2)}, u32[]{:S(2)}) collective-permute-start(bf16[1,8,16,768]{3,2,1,0:T(8,128)(2,1)S(1)} %get-tuple-element.1098), channel_id=1, source_target_pairs={{8,0},{16,8},{24,16},{9,1},{17,9},{25,17},{10,2},{18,10},{26,18},{... | collective-permute-start | bytes 589832 | tf_op jit(solution)/shard_map/while/body/eval_jaxpr/ppermute | solution.py:28
  199.6 1.3 collective-permute-start
  201.1 1.6 collective-permute-done.1
  202.7 12.8 %collective-permute-done = bf16[1,8,16,768]{3,2,1,0:T(8,128)(2,1)S(1)} collective-permute-done((bf16[1,8,16,768]{3,2,1,0:T(8,128)(2,1)S(1)}, bf16[1,8,16,768]{3,2,1,0:T(8,128)(2,1)S(1)}, u32[]{:S(2)}, u32[]{:S(2)}) %collective-permute-start) | collective-permute-done | bytes 196640 | tf_op jit(solution)/shard_map/while/body/eval_jaxpr/ppermute | solution.py:28
  215.6 4.8 %collective-permute-start.1 = (bf16[1,8,16,768]{3,2,1,0:T(8,128)(2,1)S(1)}, bf16[1,8,16,768]{3,2,1,0:T(8,128)(2,1)S(1)}, u32[]{:S(2)}, u32[]{:S(2)}) collective-permute-start(bf16[1,8,16,768]{3,2,1,0:T(8,128)(2,1)S(1)} %get-tuple-element.1098), channel_id=1, source_target_pairs={{8,0},{16,8},{24,16},{9,1},{17,9},{25,17},{10,2},{18,10},{26,18},{... | collective-permute-start | bytes 589832 | tf_op jit(solution)/shard_map/while/body/eval_jaxpr/ppermute | solution.py:28
  220.4 10.3 %conditional.4 = (bf16[1,8,16,768]{3,2,1,0:T(8,128)(2,1)S(1)}) conditional(s32[]{:T(128)} %convert_element_type.175, () %tuple.158, (pred[]{:T(512)}, bf16[4,1,8,16,768]{4,3,2,1,0:T(8,128)(2,1)S(1)}, s32[]{:T(128)}, bf16[1,8,16,768]{3,2,1,0:T(8,128)(2,1)S(1)}, s32[4]{0:T(128)S(1)}, /*index=5*/bf16[768]{0:T(1024)(128)(2,1)S(1)}, ...), branch_computations={%region_1.1_spmd, %region_2.4_spmd} | conditional | flops 617591168 | bytes 9590903 | solution.py:84
  223.0 3.5 %fusion.240 = (f32[8,16]{1,0:T(8,128)S(1)}, f32[1,8,16,768]{3,2,1,0:T(8,128)S(1)}) fusion(f32[768]{0:T(1024)S(1)} %fusion.115, f32[768]{0:T(1024)S(1)} %convert_element_type.137, f32[768]{0:T(1024)S(1)} %get-tuple-element.719, f32[768]{0:T(1024)S(1)} %get-tuple-element.720, f32[768]{0:T(1024)S(1)} %get-tuple-element.721, f32[768]{0:T(1024)S(1)} %get-tuple-element.722, ...), kind=kLoop, calls=%fused_computation.465 | loop fusion | flops 9830272 | bytes 943616 | tf_op jit(solution)/shard_map/while/body/eval_jaxpr/cond/branch_1_fun/reduce_sum | solution.py:60
  226.9 3.7 %fusion.9 = f32[128,768]{1,0:T(8,128)S(1)} fusion(bf16[1536,768]{1,0:T(8,128)(2,1)} %get-tuple-element.678, f32[1536]{0:T(1024)S(1)} %fusion.114, bf16[128,768]{1,0:T(8,128)(2,1)S(1)} %bitcast.57, bf16[1536,768]{1,0:T(8,128)(2,1)} %get-tuple-element.677), kind=kOutput, calls=%fused_computation.58 | convolution fusion | flops 605945856 | bytes 5314560 | tf_op jit(solution)/shard_map/while/body/eval_jaxpr/cond/branch_1_fun/dot_general | solution.py:70
  230.7 1.3 collective-permute-start
  232.2 13.7 %collective-permute-done = bf16[1,8,16,768]{3,2,1,0:T(8,128)(2,1)S(1)} collective-permute-done((bf16[1,8,16,768]{3,2,1,0:T(8,128)(2,1)S(1)}, bf16[1,8,16,768]{3,2,1,0:T(8,128)(2,1)S(1)}, u32[]{:S(2)}, u32[]{:S(2)}) %collective-permute-start) | collective-permute-done | bytes 196640 | tf_op jit(solution)/shard_map/while/body/eval_jaxpr/ppermute | solution.py:28
  245.9 6.9 %collective-permute-start.1 = (bf16[1,8,16,768]{3,2,1,0:T(8,128)(2,1)S(1)}, bf16[1,8,16,768]{3,2,1,0:T(8,128)(2,1)S(1)}, u32[]{:S(2)}, u32[]{:S(2)}) collective-permute-start(bf16[1,8,16,768]{3,2,1,0:T(8,128)(2,1)S(1)} %get-tuple-element.1098), channel_id=1, source_target_pairs={{8,0},{16,8},{24,16},{9,1},{17,9},{25,17},{10,2},{18,10},{26,18},{... | collective-permute-start | bytes 589832 | tf_op jit(solution)/shard_map/while/body/eval_jaxpr/ppermute | solution.py:28
  252.8 10.3 %conditional.4 = (bf16[1,8,16,768]{3,2,1,0:T(8,128)(2,1)S(1)}) conditional(s32[]{:T(128)} %convert_element_type.175, () %tuple.158, (pred[]{:T(512)}, bf16[4,1,8,16,768]{4,3,2,1,0:T(8,128)(2,1)S(1)}, s32[]{:T(128)}, bf16[1,8,16,768]{3,2,1,0:T(8,128)(2,1)S(1)}, s32[4]{0:T(128)S(1)}, /*index=5*/bf16[768]{0:T(1024)(128)(2,1)S(1)}, ...), branch_computations={%region_1.1_spmd, %region_2.4_spmd} | conditional | flops 617591168 | bytes 9590903 | solution.py:84
  255.5 3.5 %fusion.240 = (f32[8,16]{1,0:T(8,128)S(1)}, f32[1,8,16,768]{3,2,1,0:T(8,128)S(1)}) fusion(f32[768]{0:T(1024)S(1)} %fusion.115, f32[768]{0:T(1024)S(1)} %convert_element_type.137, f32[768]{0:T(1024)S(1)} %get-tuple-element.719, f32[768]{0:T(1024)S(1)} %get-tuple-element.720, f32[768]{0:T(1024)S(1)} %get-tuple-element.721, f32[768]{0:T(1024)S(1)} %get-tuple-element.722, ...), kind=kLoop, calls=%fused_computation.465 | loop fusion | flops 9830272 | bytes 943616 | tf_op jit(solution)/shard_map/while/body/eval_jaxpr/cond/branch_1_fun/reduce_sum | solution.py:60
  259.4 3.7 %fusion.9 = f32[128,768]{1,0:T(8,128)S(1)} fusion(bf16[1536,768]{1,0:T(8,128)(2,1)} %get-tuple-element.678, f32[1536]{0:T(1024)S(1)} %fusion.114, bf16[128,768]{1,0:T(8,128)(2,1)S(1)} %bitcast.57, bf16[1536,768]{1,0:T(8,128)(2,1)} %get-tuple-element.677), kind=kOutput, calls=%fused_computation.58 | convolution fusion | flops 605945856 | bytes 5314560 | tf_op jit(solution)/shard_map/while/body/eval_jaxpr/cond/branch_1_fun/dot_general | solution.py:70
  263.1 1.3 collective-permute-start
  264.6 6.1 %collective-permute-done = bf16[1,8,16,768]{3,2,1,0:T(8,128)(2,1)S(1)} collective-permute-done((bf16[1,8,16,768]{3,2,1,0:T(8,128)(2,1)S(1)}, bf16[1,8,16,768]{3,2,1,0:T(8,128)(2,1)S(1)}, u32[]{:S(2)}, u32[]{:S(2)}) %collective-permute-start) | collective-permute-done | bytes 196640 | tf_op jit(solution)/shard_map/while/body/eval_jaxpr/ppermute | solution.py:28
  (162 shorter events, 19.3 us)
Async XLA Ops:
  6.5 141.3 %all-gather.4.cloned.1.call-start = ((), (), s32[]{:S(2)}) async-start(), calls=%async_computation | async-start | bytes 2654208 | tf_op jit(solution)/shard_map/all_gather | solution.py:113
  7.3 140.6 %all-gather.6.cloned.1.call-start = ((), (), s32[]{:S(2)}) async-start(), calls=%async_computation.1 | async-start | bytes 2654208 | tf_op jit(solution)/shard_map/all_gather | solution.py:114
  8.0 139.8 %all-gather.8.cloned.1.call-start = ((), (), s32[]{:S(2)}) async-start(), calls=%async_computation.2 | async-start | bytes 2654208 | tf_op jit(solution)/shard_map/all_gather | solution.py:116
  8.1 9.0 %collective-permute-start.17 = (bf16[1,192,768]{2,1,0:T(8,128)(2,1)}, bf16[1,192,768]{2,1,0:T(8,128)(2,1)S(1)}, u32[]{:S(2)}, u32[]{:S(2)}) collective-permute-start(bf16[1,192,768]{2,1,0:T(8,128)(2,1)} %param.22), channel_id=1, source_target_pairs={{0,8},{8,0},{16,24},{24,16},{1,9},{9,1},{17,25},{25,17},{2,10},{10... | collective-permute-start | bytes 884744 | tf_op jit(solution)/shard_map/ppermute | solution.py:22
  17.1 7.9 %collective-permute-start.18 = (bf16[1,192,768]{2,1,0:T(8,128)(2,1)S(1)}, bf16[1,192,768]{2,1,0:T(8,128)(2,1)S(1)}, u32[]{:S(2)}, u32[]{:S(2)}) collective-permute-start(bf16[1,192,768]{2,1,0:T(8,128)(2,1)S(1)} %collective-permute-done.17), channel_id=1, source_target_pairs={{0,16},{8,24},{16,0},{24,8},{1,17},{9,25},{17,1},{25,9},{2,18},{10... | collective-permute-start | bytes 884744 | tf_op jit(solution)/shard_map/ppermute | solution.py:22
  25.0 0.7 copy-start.3
  25.7 7.4 %collective-permute-start.12 = (bf16[1,192,768]{2,1,0:T(8,128)(2,1)}, bf16[1,192,768]{2,1,0:T(8,128)(2,1)S(1)}, u32[]{:S(2)}, u32[]{:S(2)}) collective-permute-start(bf16[1,192,768]{2,1,0:T(8,128)(2,1)} %param.21), channel_id=1, source_target_pairs={{0,8},{8,0},{16,24},{24,16},{1,9},{9,1},{17,25},{25,17},{2,10},{10... | collective-permute-start | bytes 884744 | tf_op jit(solution)/shard_map/ppermute | solution.py:22
  33.1 6.7 %collective-permute-start.13 = (bf16[1,192,768]{2,1,0:T(8,128)(2,1)S(1)}, bf16[1,192,768]{2,1,0:T(8,128)(2,1)S(1)}, u32[]{:S(2)}, u32[]{:S(2)}) collective-permute-start(bf16[1,192,768]{2,1,0:T(8,128)(2,1)S(1)} %collective-permute-done.12), channel_id=1, source_target_pairs={{0,16},{8,24},{16,0},{24,8},{1,17},{9,25},{17,1},{25,9},{2,18},{10... | collective-permute-start | bytes 884744 | tf_op jit(solution)/shard_map/ppermute | solution.py:22
  39.9 1.6 collective-permute-start.14
  39.9 35.1 %copy-start.2 = (bf16[1,7,7,768]{3,2,1,0:T(8,128)(2,1)S(1)}, bf16[1,7,7,768]{3,2,1,0:T(8,128)(2,1)}, u32[]{:S(2)}) copy-start(bf16[1,7,7,768]{3,2,1,0:T(8,128)(2,1)} %param.17) | copy-start | bytes 225796
  39.9 35.6 %copy-start.4 = (bf16[1,768]{1,0:T(2,128)(2,1)S(1)}, bf16[1,768]{1,0:T(2,128)(2,1)}, u32[]{:S(2)}) copy-start(bf16[1,768]{1,0:T(2,128)(2,1)} %param.23) | copy-start | bytes 4612
  39.9 37.1 %copy-start.5 = (bf16[1,768]{1,0:T(2,128)(2,1)S(1)}, bf16[1,768]{1,0:T(2,128)(2,1)}, u32[]{:S(2)}) copy-start(bf16[1,768]{1,0:T(2,128)(2,1)} %param.18) | copy-start | bytes 4612
  39.9 37.6 %copy-start.6 = (bf16[1,768]{1,0:T(2,128)(2,1)S(1)}, bf16[1,768]{1,0:T(2,128)(2,1)}, u32[]{:S(2)}) copy-start(bf16[1,768]{1,0:T(2,128)(2,1)} %param.19) | copy-start | bytes 4612
  39.9 39.6 %copy-start.7 = (bf16[1,768]{1,0:T(2,128)(2,1)S(1)}, bf16[1,768]{1,0:T(2,128)(2,1)}, u32[]{:S(2)}) copy-start(bf16[1,768]{1,0:T(2,128)(2,1)} %param.20) | copy-start | bytes 4612
  41.6 26.1 %collective-permute-start.15 = (bf16[1,384,768]{2,1,0:T(8,128)(2,1)S(1)}, bf16[1,384,768]{2,1,0:T(8,128)(2,1)S(1)}, u32[]{:S(2)}, u32[]{:S(2)}) collective-permute-start(bf16[1,384,768]{2,1,0:T(8,128)(2,1)S(1)} %maximum_select_fusion.4), channel_id=1, source_target_pairs={{0,2},{1,3},{2,0},{3,1},{4,6},{5,7},{6,4},{7,5},{8,10},{9,11},{10,... | collective-permute-start | bytes 1769480 | tf_op jit(solution)/shard_map/ppermute | solution.py:11
  69.2 76.8 %collective-permute-start.16 = (bf16[1,768,768]{2,1,0:T(8,128)(2,1)}, bf16[1,768,768]{2,1,0:T(8,128)(2,1)S(1)}, u32[]{:S(2)}, u32[]{:S(2)}) collective-permute-start(bf16[1,768,768]{2,1,0:T(8,128)(2,1)} %maximum_select_fusion.2), channel_id=1, source_target_pairs={{0,4},{1,5},{2,6},{3,7},{4,0},{5,1},{6,2},{7,3},{8,12},{9,13},{10,... | collective-permute-start | bytes 3538952 | tf_op jit(solution)/shard_map/ppermute | solution.py:11
  74.9 12.9 %collective-permute-start.4 = (bf16[1,7,7,768]{3,2,1,0:T(8,128)(2,1)S(1)}, bf16[1,7,7,768]{3,2,1,0:T(8,128)(2,1)S(1)}, u32[]{:S(2)}, u32[]{:S(2)}) collective-permute-start(bf16[1,7,7,768]{3,2,1,0:T(8,128)(2,1)S(1)} %copy-done.2), channel_id=1, source_target_pairs={{0,8},{8,0},{16,24},{24,16},{1,9},{9,1},{17,25},{25,17},{2,10},{10... | collective-permute-start | bytes 225800 | tf_op jit(solution)/shard_map/ppermute | solution.py:22
  75.4 4.0 %collective-permute-start.2 = (bf16[1,768]{1,0:T(2,128)(2,1)S(1)}, bf16[1,768]{1,0:T(2,128)(2,1)S(1)}, u32[]{:S(2)}, u32[]{:S(2)}) collective-permute-start(bf16[1,768]{1,0:T(2,128)(2,1)S(1)} %copy-done.4), channel_id=1, source_target_pairs={{0,8},{8,0},{16,24},{24,16},{1,9},{9,1},{17,25},{25,17},{2,10},{10... | collective-permute-start | bytes 4616 | tf_op jit(solution)/shard_map/ppermute | solution.py:22
  77.0 3.6 %collective-permute-start.6 = (bf16[1,768]{1,0:T(2,128)(2,1)S(1)}, bf16[1,768]{1,0:T(2,128)(2,1)S(1)}, u32[]{:S(2)}, u32[]{:S(2)}) collective-permute-start(bf16[1,768]{1,0:T(2,128)(2,1)S(1)} %copy-done.5), channel_id=1, source_target_pairs={{0,8},{8,0},{16,24},{24,16},{1,9},{9,1},{17,25},{25,17},{2,10},{10... | collective-permute-start | bytes 4616 | tf_op jit(solution)/shard_map/ppermute | solution.py:22
  77.5 3.6 %collective-permute-start.8 = (bf16[1,768]{1,0:T(2,128)(2,1)S(1)}, bf16[1,768]{1,0:T(2,128)(2,1)S(1)}, u32[]{:S(2)}, u32[]{:S(2)}) collective-permute-start(bf16[1,768]{1,0:T(2,128)(2,1)S(1)} %copy-done.6), channel_id=1, source_target_pairs={{0,8},{8,0},{16,24},{24,16},{1,9},{9,1},{17,25},{25,17},{2,10},{10... | collective-permute-start | bytes 4616 | tf_op jit(solution)/shard_map/ppermute | solution.py:22
  79.4 3.6 %collective-permute-start.10 = (bf16[1,768]{1,0:T(2,128)(2,1)S(1)}, bf16[1,768]{1,0:T(2,128)(2,1)S(1)}, u32[]{:S(2)}, u32[]{:S(2)}) collective-permute-start(bf16[1,768]{1,0:T(2,128)(2,1)S(1)} %copy-done.7), channel_id=1, source_target_pairs={{0,8},{8,0},{16,24},{24,16},{1,9},{9,1},{17,25},{25,17},{2,10},{10... | collective-permute-start | bytes 4616 | tf_op jit(solution)/shard_map/ppermute | solution.py:22
  80.6 3.6 %collective-permute-start.3 = (bf16[1,768]{1,0:T(2,128)(2,1)S(1)}, bf16[1,768]{1,0:T(2,128)(2,1)S(1)}, u32[]{:S(2)}, u32[]{:S(2)}) collective-permute-start(bf16[1,768]{1,0:T(2,128)(2,1)S(1)} %collective-permute-done.2), channel_id=1, source_target_pairs={{0,16},{8,24},{16,0},{24,8},{1,17},{9,25},{17,1},{25,9},{2,18},{10... | collective-permute-start | bytes 4616 | tf_op jit(solution)/shard_map/ppermute | solution.py:22
  81.1 4.1 %collective-permute-start.7 = (bf16[1,768]{1,0:T(2,128)(2,1)S(1)}, bf16[1,768]{1,0:T(2,128)(2,1)S(1)}, u32[]{:S(2)}, u32[]{:S(2)}) collective-permute-start(bf16[1,768]{1,0:T(2,128)(2,1)S(1)} %collective-permute-done.6), channel_id=1, source_target_pairs={{0,16},{8,24},{16,0},{24,8},{1,17},{9,25},{17,1},{25,9},{2,18},{10... | collective-permute-start | bytes 4616 | tf_op jit(solution)/shard_map/ppermute | solution.py:22
  83.0 3.6 %collective-permute-start.9 = (bf16[1,768]{1,0:T(2,128)(2,1)S(1)}, bf16[1,768]{1,0:T(2,128)(2,1)S(1)}, u32[]{:S(2)}, u32[]{:S(2)}) collective-permute-start(bf16[1,768]{1,0:T(2,128)(2,1)S(1)} %collective-permute-done.8), channel_id=1, source_target_pairs={{0,16},{8,24},{16,0},{24,8},{1,17},{9,25},{17,1},{25,9},{2,18},{10... | collective-permute-start | bytes 4616 | tf_op jit(solution)/shard_map/ppermute | solution.py:22
  84.2 3.6 %collective-permute-start.11 = (bf16[1,768]{1,0:T(2,128)(2,1)S(1)}, bf16[1,768]{1,0:T(2,128)(2,1)S(1)}, u32[]{:S(2)}, u32[]{:S(2)}) collective-permute-start(bf16[1,768]{1,0:T(2,128)(2,1)S(1)} %collective-permute-done.10), channel_id=1, source_target_pairs={{0,16},{8,24},{16,0},{24,8},{1,17},{9,25},{17,1},{25,9},{2,18},{10... | collective-permute-start | bytes 4616 | tf_op jit(solution)/shard_map/ppermute | solution.py:22
  87.8 60.0 %collective-permute-start.5 = (bf16[1,7,7,768]{3,2,1,0:T(8,128)(2,1)S(1)}, bf16[1,7,7,768]{3,2,1,0:T(8,128)(2,1)S(1)}, u32[]{:S(2)}, u32[]{:S(2)}) collective-permute-start(bf16[1,7,7,768]{3,2,1,0:T(8,128)(2,1)S(1)} %collective-permute-done.4), channel_id=1, source_target_pairs={{0,16},{8,24},{16,0},{24,8},{1,17},{9,25},{17,1},{25,9},{2,18},{10... | collective-permute-start | bytes 225800 | tf_op jit(solution)/shard_map/ppermute | solution.py:22
  146.0 2.0 copy-start.1
  146.0 2.0 copy-start.8
  158.1 5.2 %collective-permute-start.1 = (bf16[1,8,16,768]{3,2,1,0:T(8,128)(2,1)S(1)}, bf16[1,8,16,768]{3,2,1,0:T(8,128)(2,1)S(1)}, u32[]{:S(2)}, u32[]{:S(2)}) collective-permute-start(bf16[1,8,16,768]{3,2,1,0:T(8,128)(2,1)S(1)} %get-tuple-element.1098), channel_id=1, source_target_pairs={{8,0},{16,8},{24,16},{9,1},{17,9},{25,17},{10,2},{18,10},{26,18},{... | collective-permute-start | bytes 589832 | tf_op jit(solution)/shard_map/while/body/eval_jaxpr/ppermute | solution.py:28
  159.5 8.0 %collective-permute-start = (bf16[1,8,16,768]{3,2,1,0:T(8,128)(2,1)S(1)}, bf16[1,8,16,768]{3,2,1,0:T(8,128)(2,1)S(1)}, u32[]{:S(2)}, u32[]{:S(2)}) collective-permute-start(bf16[1,8,16,768]{3,2,1,0:T(8,128)(2,1)S(1)} %get-tuple-element.1097), channel_id=1, source_target_pairs={{0,8},{8,16},{16,24},{1,9},{9,17},{17,25},{2,10},{10,18},{18,26},{... | collective-permute-start | bytes 589832 | tf_op jit(solution)/shard_map/while/body/eval_jaxpr/ppermute | solution.py:28
  177.5 4.6 %collective-permute-start.1 = (bf16[1,8,16,768]{3,2,1,0:T(8,128)(2,1)S(1)}, bf16[1,8,16,768]{3,2,1,0:T(8,128)(2,1)S(1)}, u32[]{:S(2)}, u32[]{:S(2)}) collective-permute-start(bf16[1,8,16,768]{3,2,1,0:T(8,128)(2,1)S(1)} %get-tuple-element.1098), channel_id=1, source_target_pairs={{8,0},{16,8},{24,16},{9,1},{17,9},{25,17},{10,2},{18,10},{26,18},{... | collective-permute-start | bytes 589832 | tf_op jit(solution)/shard_map/while/body/eval_jaxpr/ppermute | solution.py:28
  179.1 7.8 %collective-permute-start = (bf16[1,8,16,768]{3,2,1,0:T(8,128)(2,1)S(1)}, bf16[1,8,16,768]{3,2,1,0:T(8,128)(2,1)S(1)}, u32[]{:S(2)}, u32[]{:S(2)}) collective-permute-start(bf16[1,8,16,768]{3,2,1,0:T(8,128)(2,1)S(1)} %get-tuple-element.1097), channel_id=1, source_target_pairs={{0,8},{8,16},{16,24},{1,9},{9,17},{17,25},{2,10},{10,18},{18,26},{... | collective-permute-start | bytes 589832 | tf_op jit(solution)/shard_map/while/body/eval_jaxpr/ppermute | solution.py:28
  186.9 15.8 %collective-permute-start.1 = (bf16[1,8,16,768]{3,2,1,0:T(8,128)(2,1)S(1)}, bf16[1,8,16,768]{3,2,1,0:T(8,128)(2,1)S(1)}, u32[]{:S(2)}, u32[]{:S(2)}) collective-permute-start(bf16[1,8,16,768]{3,2,1,0:T(8,128)(2,1)S(1)} %get-tuple-element.1098), channel_id=1, source_target_pairs={{8,0},{16,8},{24,16},{9,1},{17,9},{25,17},{10,2},{18,10},{26,18},{... | collective-permute-start | bytes 589832 | tf_op jit(solution)/shard_map/while/body/eval_jaxpr/ppermute | solution.py:28
  199.6 15.9 %collective-permute-start = (bf16[1,8,16,768]{3,2,1,0:T(8,128)(2,1)S(1)}, bf16[1,8,16,768]{3,2,1,0:T(8,128)(2,1)S(1)}, u32[]{:S(2)}, u32[]{:S(2)}) collective-permute-start(bf16[1,8,16,768]{3,2,1,0:T(8,128)(2,1)S(1)} %get-tuple-element.1097), channel_id=1, source_target_pairs={{0,8},{8,16},{16,24},{1,9},{9,17},{17,25},{2,10},{10,18},{18,26},{... | collective-permute-start | bytes 589832 | tf_op jit(solution)/shard_map/while/body/eval_jaxpr/ppermute | solution.py:28
  215.6 16.6 %collective-permute-start.1 = (bf16[1,8,16,768]{3,2,1,0:T(8,128)(2,1)S(1)}, bf16[1,8,16,768]{3,2,1,0:T(8,128)(2,1)S(1)}, u32[]{:S(2)}, u32[]{:S(2)}) collective-permute-start(bf16[1,8,16,768]{3,2,1,0:T(8,128)(2,1)S(1)} %get-tuple-element.1098), channel_id=1, source_target_pairs={{8,0},{16,8},{24,16},{9,1},{17,9},{25,17},{10,2},{18,10},{26,18},{... | collective-permute-start | bytes 589832 | tf_op jit(solution)/shard_map/while/body/eval_jaxpr/ppermute | solution.py:28
  230.7 15.1 %collective-permute-start = (bf16[1,8,16,768]{3,2,1,0:T(8,128)(2,1)S(1)}, bf16[1,8,16,768]{3,2,1,0:T(8,128)(2,1)S(1)}, u32[]{:S(2)}, u32[]{:S(2)}) collective-permute-start(bf16[1,8,16,768]{3,2,1,0:T(8,128)(2,1)S(1)} %get-tuple-element.1097), channel_id=1, source_target_pairs={{0,8},{8,16},{16,24},{1,9},{9,17},{17,25},{2,10},{10,18},{18,26},{... | collective-permute-start | bytes 589832 | tf_op jit(solution)/shard_map/while/body/eval_jaxpr/ppermute | solution.py:28
  245.9 18.7 %collective-permute-start.1 = (bf16[1,8,16,768]{3,2,1,0:T(8,128)(2,1)S(1)}, bf16[1,8,16,768]{3,2,1,0:T(8,128)(2,1)S(1)}, u32[]{:S(2)}, u32[]{:S(2)}) collective-permute-start(bf16[1,8,16,768]{3,2,1,0:T(8,128)(2,1)S(1)} %get-tuple-element.1098), channel_id=1, source_target_pairs={{8,0},{16,8},{24,16},{9,1},{17,9},{25,17},{10,2},{18,10},{26,18},{... | collective-permute-start | bytes 589832 | tf_op jit(solution)/shard_map/while/body/eval_jaxpr/ppermute | solution.py:28
  263.1 7.6 %collective-permute-start = (bf16[1,8,16,768]{3,2,1,0:T(8,128)(2,1)S(1)}, bf16[1,8,16,768]{3,2,1,0:T(8,128)(2,1)S(1)}, u32[]{:S(2)}, u32[]{:S(2)}) collective-permute-start(bf16[1,8,16,768]{3,2,1,0:T(8,128)(2,1)S(1)} %get-tuple-element.1097), channel_id=1, source_target_pairs={{0,8},{8,16},{16,24},{1,9},{9,17},{17,25},{2,10},{10,18},{18,26},{... | collective-permute-start | bytes 589832 | tf_op jit(solution)/shard_map/while/body/eval_jaxpr/ppermute | solution.py:28
  270.7 0.9 copy-start
Sparse Core Ops, SparseCore 0:
  9.0 32.6 all-gather.3
  43.3 38.3 all-gather.5
  83.3 49.9 all-gather.7
